TPU v7x, 32 devices: a whole 2x2x4 slice. The times are simulated.
32 devices in a mesh: gx: 2 (over core), gy: 4 (over y, x), gz: 4 (over z).
Axes of the slice: x: 2, y: 2, z: 4, core: 2. Of those that a mesh axis runs over, the one named last changes fastest.
Arguments:
- basis: float32 [32, 262144], P(None, ('gx', 'gy', 'gz')), may hold values from -5.5 to 5.5
- sigma: float32 [32], replicated, may hold values from 1 to 8
- snapshots: float32 [64, 262144], P(None, ('gx', 'gy', 'gz')), may hold values from -200 to 200
Outputs:
- modes: float32 [32, 262144], P(None, ('gx', 'gy', 'gz'))
- values: float32 [32], replicated
All inputs are finite; a program needn't handle non-finite values.
Results may differ from a plain program's by a relative error of at most 0.00016.
Values sent between devices are 32-bit elements; how exact they have to be, the bound alone decides.
No kernel may reach another device: no remote copies, remote signals or barrier semaphores. Data moves between devices by JAX's collectives and lax.ppermute only.
A program may use at most 64 MiB of HBM per device.

v0:
```python
import jax
import jax.numpy as jnp
from jax import lax
from jax.sharding import PartitionSpec as P

ITERS = 4
HIGH = lax.Precision.HIGHEST


def inner(left, right, total):
    product = lax.dot_general(
        left, right, (((1,), (1,)), ((), ())), precision=HIGH, preferred_element_type=jnp.float32
    )
    return product / total


def remove(block, coeffs, basis):
    return block - jnp.dot(coeffs.T, basis, precision=HIGH)


def orthonormal(block):
    for repeat in range(2):
        factor = jnp.linalg.cholesky(jnp.dot(block.T, block, precision=HIGH))
        block = jax.scipy.linalg.solve_triangular(factor, block.T, lower=True).T
    return block


def rotate(sigma, coeffs, factor):
    modes_count = sigma.shape[0]
    fresh_count = factor.shape[0]
    upper_rows = jnp.concatenate([jnp.diag(sigma), coeffs], axis=1)
    lower_rows = jnp.concatenate(
        [jnp.zeros((fresh_count, modes_count), jnp.float32), factor], axis=1
    )
    core = jnp.concatenate([upper_rows, lower_rows], axis=0)
    square = jnp.dot(core, core.T, precision=HIGH)
    frame = jnp.eye(modes_count + fresh_count, modes_count, dtype=jnp.float32)
    for step in range(ITERS):
        frame = orthonormal(jnp.dot(square, frame, precision=HIGH))
    ritz = jnp.sum(frame * jnp.dot(square, frame, precision=HIGH), axis=0)
    return (frame, jnp.sqrt(ritz))


def per_device(basis, sigma, snapshots):
    modes_count = basis.shape[0]
    total = basis.shape[1] * lax.axis_size(("gx", "gy", "gz")) * 1.0
    correlation, first, snap_gram = lax.psum(
        (
            inner(basis, basis, total),
            inner(basis, snapshots, total),
            inner(snapshots, snapshots, total),
        ),
        ("gx", "gy", "gz"),
    )
    second = first - jnp.dot(correlation, first, precision=HIGH)
    partial_value = remove(snapshots, first, basis)
    residual = remove(partial_value, second, basis)
    joined = first + second
    cross = jnp.dot(joined.T, first, precision=HIGH)
    bent = jnp.dot(joined.T, jnp.dot(correlation, joined, precision=HIGH), precision=HIGH)
    lower = jnp.linalg.cholesky(snap_gram - cross - cross.T + bent)
    fresh = jax.scipy.linalg.solve_triangular(lower, residual, lower=True)
    frame, values = rotate(sigma, first + second, lower.T)
    modes = jnp.dot(frame[:modes_count].T, basis, precision=HIGH) + jnp.dot(
        frame[modes_count:].T, fresh, precision=HIGH
    )
    return (modes, values)


def solution(mesh):
    placed = (P(None, ("gx", "gy", "gz")), P(), P(None, ("gx", "gy", "gz")))
    return jax.shard_map(
        per_device,
        mesh=mesh,
        in_specs=placed,
        out_specs=(P(None, ("gx", "gy", "gz")), P()),
        check_vma=False,
    )
```

profile of v0, /device:TPU:0, one launch (start us, length us, event | category | flops | bytes accessed | tf_op | source)
XLA Modules:
  0.0 132.6 jit_solution(9067813681668639900)
XLA Ops:
  0.6 4.1 %convolution_multiply_fusion = f32[64,64]{0,1:T(8,128)S(1)} fusion(f32[64,8192]{1,0:T(8,128)} %param.8), kind=kOutput, calls=%fused_computation.4 | convolution fusion | flops 402657280 | bytes 2113536 | tf_op jit(solution)/shard_map/dot_general | solution.py:11
  8.2 42.8 %all-reduce.1 = (f32[32,64]{1,0:T(8,128)S(1)}, f32[32,32]{1,0:T(8,128)S(1)}, f32[64,64]{0,1:T(8,128)S(1)}) all-reduce(f32[32,64]{1,0:T(8,128)S(1)} %convolution_multiply_fusion.3, f32[32,32]{1,0:T(8,128)S(1)} %convolution_multiply_fusion.2, ...), channel_id=1, replica_groups=mesh['gx'=2,'gy'=4,'gz'=4] {'gx','gy','gz'}, use_global_device_ids=true, to_apply=%region_0.0 | all-reduce | flops 7168 | bytes 57344 | tf_op jit(solution)/shard_map/psum | solution.py:47
  51.9 5.8 %cholesky.34 = f32[64,64]{1,0:T(8,128)S(1)} custom-call(f32[64,64]{1,0:T(8,128)S(1)} %fusion.7), custom_call_target="Cholesky" | custom-call | tf_op jit(solution)/shard_map/jit(cholesky)/cholesky | solution.py:61
  59.1 4.9 %custom-call.12 = f32[1,64,64]{1,2,0:T(8,128)S(1)} custom-call(f32[1,64,64]{2,1,0:T(8,128)S(1)} %get-tuple-element.7), custom_call_target="InvertDiagBlocksLowerTriangular" | custom-call | tf_op jit(solution)/shard_map/jit(_solve_triangular)/triangular_solve | solution.py:62
  64.0 1.9 %convolution_subtract_fusion.1 = f32[64,8192]{1,0:T(8,128)S(1)} fusion(f32[64,8192]{1,0:T(8,128)S(1)} %copy-done.1, f32[32,64]{1,0:T(8,128)S(1)} %get-tuple-element.4, f32[32,8192]{1,0:T(8,128)S(1)} %copy-done), kind=kOutput, calls=%fused_computation.1 | convolution fusion | flops 201850880 | bytes 5251072 | tf_op jit(solution)/shard_map/dot_general | solution.py:18
  65.9 1.9 %convolution_subtract_fusion = f32[64,8192]{1,0:T(8,128)S(1)} fusion(f32[64,8192]{1,0:T(8,128)S(1)} %convolution_subtract_fusion.1, f32[32,64]{1,0:T(8,128)S(1)} %get-tuple-element.10, f32[32,8192]{1,0:T(8,128)S(1)} %copy-done), kind=kOutput, calls=%fused_computation | convolution fusion | flops 201850880 | bytes 5251072 | tf_op jit(solution)/shard_map/dot_general | solution.py:18
  67.8 1.9 %fusion.5 = f32[64,8192]{1,0:T(8,128)S(1)} fusion(f32[64,8192]{1,0:T(8,128)S(1)} %convolution_subtract_fusion, f32[1,64,64]{1,2,0:T(8,128)S(1)} %custom-call.12), kind=kOutput, calls=%fused_computation.17 | convolution fusion | flops 402653184 | bytes 4210688 | tf_op jit(solution)/shard_map/jit(_solve_triangular)/triangular_solve | solution.py:62
  70.7 2.9 %cholesky.172 = f32[32,32]{1,0:T(8,128)S(1)} custom-call(f32[32,32]{1,0:T(8,128)S(1)} %fusion.49), custom_call_target="Cholesky" | custom-call | tf_op jit(solution)/shard_map/jit(cholesky)/cholesky | solution.py:23
  75.0 2.4 %custom-call.20 = f32[1,32,32]{1,2,0:T(8,128)S(1)} custom-call(f32[1,32,32]{2,1,0:T(8,128)S(1)} %fusion.11), custom_call_target="InvertDiagBlocksLowerTriangular" | custom-call | tf_op jit(solution)/shard_map/jit(_solve_triangular)/triangular_solve | solution.py:24
  77.9 2.9 %cholesky.183 = f32[32,32]{1,0:T(8,128)S(1)} custom-call(f32[32,32]{1,0:T(8,128)S(1)} %fusion.45), custom_call_target="Cholesky" | custom-call | tf_op jit(solution)/shard_map/jit(cholesky)/cholesky | solution.py:23
  82.2 2.4 %custom-call.21 = f32[1,32,32]{1,2,0:T(8,128)S(1)} custom-call(f32[1,32,32]{2,1,0:T(8,128)S(1)} %fusion.12), custom_call_target="InvertDiagBlocksLowerTriangular" | custom-call | tf_op jit(solution)/shard_map/jit(_solve_triangular)/triangular_solve | solution.py:24
  85.3 2.9 %cholesky.194 = f32[32,32]{1,0:T(8,128)S(1)} custom-call(f32[32,32]{1,0:T(8,128)S(1)} %fusion.42), custom_call_target="Cholesky" | custom-call | tf_op jit(solution)/shard_map/jit(cholesky)/cholesky | solution.py:23
  89.5 2.4 %custom-call.22 = f32[1,32,32]{1,2,0:T(8,128)S(1)} custom-call(f32[1,32,32]{2,1,0:T(8,128)S(1)} %fusion.13), custom_call_target="InvertDiagBlocksLowerTriangular" | custom-call | tf_op jit(solution)/shard_map/jit(_solve_triangular)/triangular_solve | solution.py:24
  92.5 2.9 %cholesky.205 = f32[32,32]{1,0:T(8,128)S(1)} custom-call(f32[32,32]{1,0:T(8,128)S(1)} %fusion.38), custom_call_target="Cholesky" | custom-call | tf_op jit(solution)/shard_map/jit(cholesky)/cholesky | solution.py:23
  96.7 2.4 %custom-call.23 = f32[1,32,32]{1,2,0:T(8,128)S(1)} custom-call(f32[1,32,32]{2,1,0:T(8,128)S(1)} %fusion.14), custom_call_target="InvertDiagBlocksLowerTriangular" | custom-call | tf_op jit(solution)/shard_map/jit(_solve_triangular)/triangular_solve | solution.py:24
  99.8 2.9 %cholesky.216 = f32[32,32]{1,0:T(8,128)S(1)} custom-call(f32[32,32]{1,0:T(8,128)S(1)} %fusion.35), custom_call_target="Cholesky" | custom-call | tf_op jit(solution)/shard_map/jit(cholesky)/cholesky | solution.py:23
  104.1 2.4 %custom-call.24 = f32[1,32,32]{1,2,0:T(8,128)S(1)} custom-call(f32[1,32,32]{2,1,0:T(8,128)S(1)} %fusion.15), custom_call_target="InvertDiagBlocksLowerTriangular" | custom-call | tf_op jit(solution)/shard_map/jit(_solve_triangular)/triangular_solve | solution.py:24
  107.0 2.9 %cholesky.227 = f32[32,32]{1,0:T(8,128)S(1)} custom-call(f32[32,32]{1,0:T(8,128)S(1)} %fusion.31), custom_call_target="Cholesky" | custom-call | tf_op jit(solution)/shard_map/jit(cholesky)/cholesky | solution.py:23
  111.3 2.6 %custom-call.25 = f32[1,32,32]{1,2,0:T(8,128)S(1)} custom-call(f32[1,32,32]{2,1,0:T(8,128)S(1)} %fusion.16), custom_call_target="InvertDiagBlocksLowerTriangular" | custom-call | tf_op jit(solution)/shard_map/jit(_solve_triangular)/triangular_solve | solution.py:24
  114.5 2.9 %cholesky.238 = f32[32,32]{1,0:T(8,128)S(1)} custom-call(f32[32,32]{1,0:T(8,128)S(1)} %fusion.28), custom_call_target="Cholesky" | custom-call | tf_op jit(solution)/shard_map/jit(cholesky)/cholesky | solution.py:23
  118.8 2.4 %custom-call.26 = f32[1,32,32]{1,2,0:T(8,128)S(1)} custom-call(f32[1,32,32]{2,1,0:T(8,128)S(1)} %fusion.17), custom_call_target="InvertDiagBlocksLowerTriangular" | custom-call | tf_op jit(solution)/shard_map/jit(_solve_triangular)/triangular_solve | solution.py:24
  121.7 2.9 %cholesky.249 = f32[32,32]{1,0:T(8,128)S(1)} custom-call(f32[32,32]{1,0:T(8,128)S(1)} %fusion.24), custom_call_target="Cholesky" | custom-call | tf_op jit(solution)/shard_map/jit(cholesky)/cholesky | solution.py:23
  125.9 2.4 %custom-call.27 = f32[1,32,32]{1,2,0:T(8,128)S(1)} custom-call(f32[1,32,32]{2,1,0:T(8,128)S(1)} %fusion.18), custom_call_target="InvertDiagBlocksLowerTriangular" | custom-call | tf_op jit(solution)/shard_map/jit(_solve_triangular)/triangular_solve | solution.py:24
  129.6 2.1 %convolution_add_fusion = f32[32,8192]{1,0:T(8,128)} fusion(f32[32,8192]{1,0:T(8,128)S(1)} %fusion.20, f32[64,8192]{1,0:T(8,128)S(1)} %fusion.5, f32[96,32]{0,1:T(8,128)S(1)} %bitcast.152), kind=kOutput, calls=%fused_computation.2 | convolution fusion | flops 201588736 | bytes 4206592 | tf_op jit(solution)/shard_map/dot_general | solution.py:64
  (85 shorter events, 23.1 us)
Async XLA Ops:
  0.6 4.1 %copy-start = (f32[32,8192]{1,0:T(8,128)S(1)}, f32[32,8192]{1,0:T(8,128)}, u32[]{:S(2)}) copy-start(f32[32,8192]{1,0:T(8,128)} %param.6) | copy-start | bytes 3145732
  4.8 1.6 %copy-start.1 = (f32[64,8192]{1,0:T(8,128)S(1)}, f32[64,8192]{1,0:T(8,128)}, u32[]{:S(2)}) copy-start(f32[64,8192]{1,0:T(8,128)} %param.8) | copy-start | bytes 6291460
  67.8 1.9 %copy-start.2 = (f32[32]{0:T(128)S(1)}, f32[32]{0:T(128)}, u32[]{:S(2)}) copy-start(f32[32]{0:T(128)} %param.7) | copy-start | bytes 388
where the time goes:
time: 133 us
  other arithmetic  65.9 us (50%)
  blocking collectives  42.8 us (32%)
  matrix products  20.8 us (16%)
  local copies, waits for them, and re-layouts  1.98 us (1%)
    psum x1, blocking collectives, per_device(): lax.psum((inner(basis, basis, total), inner(basis, snapshots, total), inn...  42.8 us
    another operation x24, other arithmetic, orthonormal(): factor = jnp.linalg.cholesky(jnp.dot(block.T, block, precision=HIGH))  28.8 us
    another operation x16, other arithmetic, orthonormal(): block = jax.scipy.linalg.solve_triangular(factor, block.T, lower=True).T  24.8 us
    dot_general x3, matrix products, inner(): lax.dot_general(left, right, (((1,), (1,)), ((), ())), precision=HIGH, pr...  6.85 us
    another operation x3, other arithmetic, per_device(): lower = jnp.linalg.cholesky(snap_gram - cross - cross.T + bent)  6.52 us
    another operation x2, other arithmetic, per_device(): fresh = jax.scipy.linalg.solve_triangular(lower, residual, lower=True)  5.55 us
    dot_general x2, matrix products, remove(): return block - jnp.dot(coeffs.T, basis, precision=HIGH)  3.74 us

commit v1 on v0

--- a/solution.py
+++ b/solution.py
@@ -45,12 +45,15 @@
     modes_count = basis.shape[0]
     total = basis.shape[1] * lax.axis_size(("gx", "gy", "gz")) * 1.0
     correlation, first, snap_gram = lax.psum(
-        (
-            inner(basis, basis, total),
-            inner(basis, snapshots, total),
-            inner(snapshots, snapshots, total),
+        lax.psum(
+            (
+                inner(basis, basis, total),
+                inner(basis, snapshots, total),
+                inner(snapshots, snapshots, total),
+            ),
+            ("gy", "gz"),
         ),
-        ("gx", "gy", "gz"),
+        "gx",
     )
     second = first - jnp.dot(correlation, first, precision=HIGH)
     partial_value = remove(snapshots, first, basis)

time: 133 us -> 173 us (1.30)
  blocking collectives: 42.8 us -> 82.8 us
    psum x1, blocking collectives: 42.8 us -> 79.1 us  [per_device(): lax.psum((inner(basis, basis, total), inner(basis, snapshots, total), inn...]
    psum x0 -> x1, blocking collectives: none -> 3.77 us  [per_device(): lax.psum(lax.psum((inner(basis, basis, total), inner(basis, snapshots, to...]
where the time goes in v1:
time: 173 us
  blocking collectives  82.8 us (48%)
  other arithmetic  65.9 us (38%)
  matrix products  20.8 us (12%)
  local copies, waits for them, and re-layouts  1.98 us (1%)
    psum x1, blocking collectives, per_device(): lax.psum((inner(basis, basis, total), inner(basis, snapshots, total), inn...  79.1 us
    another operation x24, other arithmetic, orthonormal(): factor = jnp.linalg.cholesky(jnp.dot(block.T, block, precision=HIGH))  28.8 us
    another operation x16, other arithmetic, orthonormal(): block = jax.scipy.linalg.solve_triangular(factor, block.T, lower=True).T  24.8 us
    dot_general x3, matrix products, inner(): lax.dot_general(left, right, (((1,), (1,)), ((), ())), precision=HIGH, pr...  6.85 us
    another operation x3, other arithmetic, per_device(): lower = jnp.linalg.cholesky(snap_gram - cross - cross.T + bent)  6.52 us
    another operation x2, other arithmetic, per_device(): fresh = jax.scipy.linalg.solve_triangular(lower, residual, lower=True)  5.55 us
    psum x1, blocking collectives, per_device(): lax.psum(lax.psum((inner(basis, basis, total), inner(basis, snapshots, to...  3.77 us
    dot_general x2, matrix products, remove(): return block - jnp.dot(coeffs.T, basis, precision=HIGH)  3.74 us

profile of v1, /device:TPU:0, one launch (start us, length us, event | category | flops | bytes accessed | tf_op | source)
XLA Modules:
  0.0 172.6 jit_solution(14223379268992370103)
XLA Ops:
  0.6 4.1 %convolution_multiply_fusion = f32[64,64]{0,1:T(8,128)S(1)} fusion(f32[64,8192]{1,0:T(8,128)} %param.8), kind=kOutput, calls=%fused_computation.4 | convolution fusion | flops 402657280 | bytes 2113536 | tf_op jit(solution)/shard_map/dot_general | solution.py:11
  8.2 79.1 %all-reduce.1 = (f32[32,64]{1,0:T(8,128)S(1)}, f32[32,32]{1,0:T(8,128)S(1)}, f32[64,64]{0,1:T(8,128)S(1)}) all-reduce(f32[32,64]{1,0:T(8,128)S(1)} %convolution_multiply_fusion.3, f32[32,32]{1,0:T(8,128)S(1)} %convolution_multiply_fusion.2, f32[64,64]{0,1:T(8,128)S(1)} %convolution_multiply_fusion), channel_id=1, replica_groups=mesh['gx'=2,'gy'=4,'gz'=4] {'gy','gz'}, use_global_device_ids=true, to_apply=%region_0.0 | all-reduce | flops 7168 | bytes 57344 | tf_op jit(solution)/shard_map/psum | solution.py:48
  87.2 3.8 %all-reduce.2 = (f32[32,64]{1,0:T(8,128)S(1)}, f32[32,32]{1,0:T(8,128)S(1)}, f32[64,64]{0,1:T(8,128)S(1)}) all-reduce(f32[32,64]{1,0:T(8,128)S(1)} %get-tuple-element.4, f32[32,32]{1,0:T(8,128)S(1)} %get-tuple-element.5, f32[64,64]{0,1:T(8,128)S(1)} %get-tuple-element.6), channel_id=1, replica_groups=mesh['gx'=2,'gy'=4,'gz'=4] {'gx'}, use_global_device_ids=true, to_apply=%region_1.0 | all-reduce | flops 7168 | bytes 57344 | tf_op jit(solution)/shard_map/psum | solution.py:47
  92.0 5.8 %cholesky.34 = f32[64,64]{1,0:T(8,128)S(1)} custom-call(f32[64,64]{1,0:T(8,128)S(1)} %fusion.7), custom_call_target="Cholesky" | custom-call | tf_op jit(solution)/shard_map/jit(cholesky)/cholesky | solution.py:64
  99.2 4.9 %custom-call.12 = f32[1,64,64]{1,2,0:T(8,128)S(1)} custom-call(f32[1,64,64]{2,1,0:T(8,128)S(1)} %get-tuple-element.10), custom_call_target="InvertDiagBlocksLowerTriangular" | custom-call | tf_op jit(solution)/shard_map/jit(_solve_triangular)/triangular_solve | solution.py:65
  104.1 1.9 %convolution_subtract_fusion.1 = f32[64,8192]{1,0:T(8,128)S(1)} fusion(f32[64,8192]{1,0:T(8,128)S(1)} %copy-done.1, f32[32,64]{1,0:T(8,128)S(1)} %get-tuple-element.7, f32[32,8192]{1,0:T(8,128)S(1)} %copy-done), kind=kOutput, calls=%fused_computation.1 | convolution fusion | flops 201850880 | bytes 5251072 | tf_op jit(solution)/shard_map/dot_general | solution.py:18
  107.8 1.9 %fusion.5 = f32[64,8192]{1,0:T(8,128)S(1)} fusion(f32[64,8192]{1,0:T(8,128)S(1)} %convolution_subtract_fusion, f32[1,64,64]{1,2,0:T(8,128)S(1)} %custom-call.12), kind=kOutput, calls=%fused_computation.17 | convolution fusion | flops 402653184 | bytes 4210688 | tf_op jit(solution)/shard_map/jit(_solve_triangular)/triangular_solve | solution.py:65
  110.8 2.9 %cholesky.172 = f32[32,32]{1,0:T(8,128)S(1)} custom-call(f32[32,32]{1,0:T(8,128)S(1)} %fusion.49), custom_call_target="Cholesky" | custom-call | tf_op jit(solution)/shard_map/jit(cholesky)/cholesky | solution.py:23
  115.1 2.4 %custom-call.20 = f32[1,32,32]{1,2,0:T(8,128)S(1)} custom-call(f32[1,32,32]{2,1,0:T(8,128)S(1)} %fusion.11), custom_call_target="InvertDiagBlocksLowerTriangular" | custom-call | tf_op jit(solution)/shard_map/jit(_solve_triangular)/triangular_solve | solution.py:24
  118.0 2.9 %cholesky.183 = f32[32,32]{1,0:T(8,128)S(1)} custom-call(f32[32,32]{1,0:T(8,128)S(1)} %fusion.45), custom_call_target="Cholesky" | custom-call | tf_op jit(solution)/shard_map/jit(cholesky)/cholesky | solution.py:23
  122.2 2.4 %custom-call.21 = f32[1,32,32]{1,2,0:T(8,128)S(1)} custom-call(f32[1,32,32]{2,1,0:T(8,128)S(1)} %fusion.12), custom_call_target="InvertDiagBlocksLowerTriangular" | custom-call | tf_op jit(solution)/shard_map/jit(_solve_triangular)/triangular_solve | solution.py:24
  125.4 2.9 %cholesky.194 = f32[32,32]{1,0:T(8,128)S(1)} custom-call(f32[32,32]{1,0:T(8,128)S(1)} %fusion.42), custom_call_target="Cholesky" | custom-call | tf_op jit(solution)/shard_map/jit(cholesky)/cholesky | solution.py:23
  129.6 2.4 %custom-call.22 = f32[1,32,32]{1,2,0:T(8,128)S(1)} custom-call(f32[1,32,32]{2,1,0:T(8,128)S(1)} %fusion.13), custom_call_target="InvertDiagBlocksLowerTriangular" | custom-call | tf_op jit(solution)/shard_map/jit(_solve_triangular)/triangular_solve | solution.py:24
  132.5 2.9 %cholesky.205 = f32[32,32]{1,0:T(8,128)S(1)} custom-call(f32[32,32]{1,0:T(8,128)S(1)} %fusion.38), custom_call_target="Cholesky" | custom-call | tf_op jit(solution)/shard_map/jit(cholesky)/cholesky | solution.py:23
  136.8 2.4 %custom-call.23 = f32[1,32,32]{1,2,0:T(8,128)S(1)} custom-call(f32[1,32,32]{2,1,0:T(8,128)S(1)} %fusion.14), custom_call_target="InvertDiagBlocksLowerTriangular" | custom-call | tf_op jit(solution)/shard_map/jit(_solve_triangular)/triangular_solve | solution.py:24
  139.9 2.9 %cholesky.216 = f32[32,32]{1,0:T(8,128)S(1)} custom-call(f32[32,32]{1,0:T(8,128)S(1)} %fusion.35), custom_call_target="Cholesky" | custom-call | tf_op jit(solution)/shard_map/jit(cholesky)/cholesky | solution.py:23
  144.2 2.4 %custom-call.24 = f32[1,32,32]{1,2,0:T(8,128)S(1)} custom-call(f32[1,32,32]{2,1,0:T(8,128)S(1)} %fusion.15), custom_call_target="InvertDiagBlocksLowerTriangular" | custom-call | tf_op jit(solution)/shard_map/jit(_solve_triangular)/triangular_solve | solution.py:24
  147.1 2.9 %cholesky.227 = f32[32,32]{1,0:T(8,128)S(1)} custom-call(f32[32,32]{1,0:T(8,128)S(1)} %fusion.31), custom_call_target="Cholesky" | custom-call | tf_op jit(solution)/shard_map/jit(cholesky)/cholesky | solution.py:23
  151.3 2.6 %custom-call.25 = f32[1,32,32]{1,2,0:T(8,128)S(1)} custom-call(f32[1,32,32]{2,1,0:T(8,128)S(1)} %fusion.16), custom_call_target="InvertDiagBlocksLowerTriangular" | custom-call | tf_op jit(solution)/shard_map/jit(_solve_triangular)/triangular_solve | solution.py:24
  154.6 2.9 %cholesky.238 = f32[32,32]{1,0:T(8,128)S(1)} custom-call(f32[32,32]{1,0:T(8,128)S(1)} %fusion.28), custom_call_target="Cholesky" | custom-call | tf_op jit(solution)/shard_map/jit(cholesky)/cholesky | solution.py:23
  158.8 2.4 %custom-call.26 = f32[1,32,32]{1,2,0:T(8,128)S(1)} custom-call(f32[1,32,32]{2,1,0:T(8,128)S(1)} %fusion.17), custom_call_target="InvertDiagBlocksLowerTriangular" | custom-call | tf_op jit(solution)/shard_map/jit(_solve_triangular)/triangular_solve | solution.py:24
  161.7 2.9 %cholesky.249 = f32[32,32]{1,0:T(8,128)S(1)} custom-call(f32[32,32]{1,0:T(8,128)S(1)} %fusion.24), custom_call_target="Cholesky" | custom-call | tf_op jit(solution)/shard_map/jit(cholesky)/cholesky | solution.py:23
  166.0 2.4 %custom-call.27 = f32[1,32,32]{1,2,0:T(8,128)S(1)} custom-call(f32[1,32,32]{2,1,0:T(8,128)S(1)} %fusion.18), custom_call_target="InvertDiagBlocksLowerTriangular" | custom-call | tf_op jit(solution)/shard_map/jit(_solve_triangular)/triangular_solve | solution.py:24
  169.7 2.1 %convolution_add_fusion = f32[32,8192]{1,0:T(8,128)} fusion(f32[32,8192]{1,0:T(8,128)S(1)} %fusion.20, f32[64,8192]{1,0:T(8,128)S(1)} %fusion.5, f32[96,32]{0,1:T(8,128)S(1)} %bitcast.152), kind=kOutput, calls=%fused_computation.2 | convolution fusion | flops 201588736 | bytes 4206592 | tf_op jit(solution)/shard_map/dot_general | solution.py:67
  (86 shorter events, 24.9 us)
Async XLA Ops:
  0.6 4.1 %copy-start = (f32[32,8192]{1,0:T(8,128)S(1)}, f32[32,8192]{1,0:T(8,128)}, u32[]{:S(2)}) copy-start(f32[32,8192]{1,0:T(8,128)} %param.6) | copy-start | bytes 3145732
  4.8 1.6 copy-start.1
  107.8 1.9 %copy-start.2 = (f32[32]{0:T(128)S(1)}, f32[32]{0:T(128)}, u32[]{:S(2)}) copy-start(f32[32]{0:T(128)} %param.7) | copy-start | bytes 388
